TPU v7x, 32 devices: a whole 2x2x4 slice. The times are simulated.
32 devices in a mesh: dp: 4 (over y, core), expert: 8 (over z, x).
Axes of the slice: x: 2, y: 2, z: 4, core: 2. Of those that a mesh axis runs over, the one named last changes fastest.
Arguments:
- patches: bfloat16 [16384, 768], P(('dp', 'expert')), may hold values from -6 to 6
- owner_slot: int32 [128], P(('dp', 'expert')), may hold values from 0 to 127, as said below
- segment_ids: int32 [16384], P(('dp', 'expert')), may hold values from 0 to 127, as said below
- block_mask: int32 [128, 4], P(('dp', 'expert')), may hold values from 0 to 1, as said below
- project_in: bfloat16 [768, 2304], replicated, may hold values from -30 to 30
- project_out: bfloat16 [768, 768], replicated, may hold values from -0.21875 to 0.21875
- slot_keys: bfloat16 [768, 32], replicated, may hold values from -30 to 30
- expert_in: bfloat16 [32, 768, 3072], P(('dp', 'expert')), may hold values from -0.21875 to 0.21875
- expert_out: bfloat16 [32, 3072, 768], P(('dp', 'expert')), may hold values from -0.109375 to 0.109375
Outputs:
- layer_out: bfloat16 [16384, 768], P(('dp', 'expert'))
Inputs may be any that keep to these rules, and one draw needn't show every extreme that they name: A permutation of the 128 blocks. Devices are numbered over dp then expert, and block g is read by device g // 4; it goes to device owner_slot[g] // 4, which has the same index along expert. Each reading device sends exactly 1 block to each of 4 distinct devices along dp, and each device receives exactly 4 blocks. `segment_ids`: Non-decreasing; the rows of run o (rows o * 512 to o * 512 + 511) carry the image numbers o * 4 to o * 4 + 3, each on one row or more. block_mask[o * 4 + a, b] is 1 when blocks a and b of run o hold rows of a common image, else 0.
All inputs are finite; a program needn't handle non-finite values.
Results may differ from a plain program's by a relative error of at most 0.0095.
The roundings to bfloat16 on the way count: a program that leaves them out, or rounds other values in their place, can miss the bound.
Values may be sent and summed in bfloat16 or wider, within the bound.
No kernel may reach another device: no remote copies, remote signals or barrier semaphores. Data moves between devices by JAX's collectives and lax.ppermute only.
A program may use at most 128 MiB of HBM per device.

v0:
```python
import jax
import jax.numpy as jnp
from jax import lax
from jax.sharding import PartitionSpec as P

HEADS = 12
HEAD = 64
EPS = 1e-06
NEGATIVE = -1e30


def layer_norm(values):
    values = values.astype(jnp.float32)
    centred = values - jnp.mean(values, axis=-1, keepdims=True)
    variance = jnp.mean(centred * centred, axis=-1, keepdims=True)
    return centred * lax.rsqrt(variance + EPS)


def per_device(
    patches,
    owner_slot,
    segment_ids,
    block_mask,
    project_in,
    project_out,
    slot_keys,
    expert_in,
    expert_out,
):
    width = patches.shape[1]
    blk_count = owner_slot.shape[0]
    tok_count = patches.shape[0]
    block_rows = tok_count // blk_count
    data_count = lax.axis_size("dp")
    column_count = lax.axis_size("expert")
    peer_cap = max(1, blk_count // data_count)
    slot_total = data_count * peer_cap
    highest = lax.Precision.HIGHEST
    target_data = owner_slot // blk_count // column_count
    target_place = owner_slot % blk_count
    to_peer = (target_data[:, None] == jnp.arange(data_count, dtype=jnp.int32)[None, :]).astype(
        jnp.int32
    )
    peer_rank = jnp.sum((jnp.cumsum(to_peer, axis=0) - 1) * to_peer, axis=1)
    send_index = target_data * peer_cap + peer_rank
    route = send_index[None, :] == jnp.arange(slot_total, dtype=jnp.int32)[:, None]
    flat_blocks = patches.reshape(blk_count, block_rows * width)
    send_rows = jnp.dot(
        route.astype(jnp.bfloat16), flat_blocks, preferred_element_type=jnp.float32
    ).astype(jnp.bfloat16)
    send_place = jnp.sum(route.astype(jnp.int32) * (target_place[None, :] + 1), axis=1) - 1
    arrived_rows, arrived_place = (
        lax.all_to_all(
            send_rows.reshape(data_count, peer_cap, block_rows * width),
            "dp",
            split_axis=0,
            concat_axis=0,
            tiled=True,
        ),
        lax.all_to_all(
            send_place.reshape(data_count, peer_cap), "dp", split_axis=0, concat_axis=0, tiled=True
        ),
    )
    placing = (
        arrived_place.reshape(1, slot_total) == jnp.arange(blk_count, dtype=jnp.int32)[:, None]
    ).astype(jnp.bfloat16)
    ordered = jnp.dot(
        placing,
        arrived_rows.reshape(slot_total, block_rows * width),
        preferred_element_type=jnp.float32,
    )
    ordered = ordered.astype(jnp.bfloat16).reshape(tok_count, width)
    normed = layer_norm(ordered).astype(jnp.bfloat16)
    joint = jnp.dot(normed, project_in, preferred_element_type=jnp.float32).astype(jnp.bfloat16)
    queries = joint[:, :width].reshape(tok_count, HEADS, HEAD)
    key_rows = joint[:, width : 2 * width].reshape(tok_count, HEADS, HEAD)
    value_rows = joint[:, 2 * width :].reshape(tok_count, HEADS, HEAD)
    linked_blocks = jnp.broadcast_to(
        block_mask[:, None, :, None] == 1, (blk_count, block_rows, blk_count, block_rows)
    ).reshape(tok_count, tok_count)
    linked = linked_blocks & (segment_ids[:, None] == segment_ids[None, :])
    scores = jnp.einsum(
        "qhd,khd->hqk", queries, key_rows, preferred_element_type=jnp.float32
    ) * HEAD ** (-0.5)
    scores = jnp.where(linked[None], scores, NEGATIVE)
    raised = jnp.exp(scores - jnp.max(scores, axis=2, keepdims=True))
    weights = (raised / jnp.sum(raised, axis=2, keepdims=True)).astype(jnp.bfloat16)
    attended = jnp.einsum("hqk,khd->qhd", weights, value_rows, preferred_element_type=jnp.float32)
    pieces = attended.astype(jnp.bfloat16).reshape(-1, width)
    hidden = (
        ordered.astype(jnp.float32)
        + jnp.dot(pieces, project_out, preferred_element_type=jnp.float32)
    ).astype(jnp.bfloat16)
    moe_normed = layer_norm(hidden).astype(jnp.bfloat16)
    logits = jnp.dot(moe_normed, slot_keys, preferred_element_type=jnp.float32)
    local_image = segment_ids % blk_count
    member = local_image[None, :] == jnp.arange(blk_count, dtype=jnp.int32)[:, None]
    member_float = member.astype(jnp.float32)
    column_max = jnp.max(jnp.where(member[:, :, None], logits[None], NEGATIVE), axis=1)
    row_shift = jnp.dot(member_float.T, column_max, precision=highest)
    raised_slots = jnp.exp(logits - row_shift)
    totals = jnp.dot(member_float, raised_slots, precision=highest)
    row_totals = jnp.dot(member_float.T, totals, precision=highest)
    dispatch = (raised_slots / row_totals).astype(jnp.bfloat16)
    masked = jnp.where(member[:, :, None], dispatch[None], jnp.zeros((), jnp.bfloat16))
    slot_in = jnp.einsum(
        "ste,td->sed", masked, moe_normed, preferred_element_type=jnp.float32
    ).astype(jnp.bfloat16)
    slot_raised = jnp.exp(logits - jnp.max(logits, axis=1, keepdims=True))
    combine = (slot_raised / jnp.sum(slot_raised, axis=1, keepdims=True)).astype(jnp.bfloat16)
    arrived = lax.all_to_all(slot_in, ("dp", "expert"), split_axis=1, concat_axis=0, tiled=True)
    inner = jnp.einsum("rkd,kdh->rkh", arrived, expert_in, preferred_element_type=jnp.float32)
    inner = jax.nn.gelu(inner, approximate=False).astype(jnp.bfloat16)
    produced = jnp.einsum(
        "rkh,khd->rkd", inner, expert_out, preferred_element_type=jnp.float32
    ).astype(jnp.bfloat16)
    returned = lax.all_to_all(produced, ("dp", "expert"), split_axis=0, concat_axis=1, tiled=True)
    masked_combine = jnp.where(member[:, :, None], combine[None], jnp.zeros((), jnp.bfloat16))
    mixture = jnp.einsum(
        "ste,sed->td", masked_combine, returned, preferred_element_type=jnp.float32
    )
    return (hidden.astype(jnp.float32) + mixture).astype(jnp.bfloat16)


def solution(mesh):
    in_specs = (
        P(("dp", "expert"), None),
        P(("dp", "expert")),
        P(("dp", "expert")),
        P(("dp", "expert"), None),
        P(),
        P(),
        P(),
        P(("dp", "expert"), None, None),
        P(("dp", "expert"), None, None),
    )
    out_specs = P(("dp", "expert"), None)
    return jax.shard_map(
        per_device, mesh=mesh, in_specs=in_specs, out_specs=out_specs, check_vma=False
    )
```

profile of v0, /device:TPU:0, one launch (start us, length us, event | category | flops | bytes accessed | tf_op | source)
XLA Modules:
  0.0 129.7 jit_solution(2665563277811735004)
XLA Ops:
  1.9 4.3 %all-to-all-start = ((s32[4,1,1]{2,1,0:T(1,128)}), s32[4,1,1]{2,1,0:T(1,128)S(1)}, u32[]{:S(2)}, u32[]{:S(2)}) async-start(s32[4,1,1]{2,1,0:T(1,128)} %copy.42), calls=%async_computation | async-start | bytes 4096 | tf_op jit(solution)/shard_map/all_to_all | solution.py:60
  6.2 2.6 %reshape.151 = bf16[4,98304]{1,0:T(4,128)(2,1)} reshape(bf16[512,768]{1,0:T(8,128)(2,1)} %param.9) | data formatting | bytes 1572864 | tf_op jit(solution)/shard_map/reshape | solution.py:47
  8.8 2.6 %fusion.2 = bf16[4,1,98304]{2,0,1:T(4,128)(2,1)} fusion(bf16[4,98304]{1,0:T(4,128)(2,1)} %reshape.151, s32[4]{0:T(128)S(1)} %add.54), kind=kOutput, calls=%fused_computation.4 | convolution fusion | flops 3538960 | bytes 1572880 | tf_op jit(solution)/shard_map/dot_general | solution.py:48
  11.9 3.6 %reduce.2 = bf16[4,98304]{1,0:T(4,128)(2,1)} reduce(bf16[4,1,98304]{2,0,1:T(4,128)(2,1)} %fusion.2, bf16[]{:T(256)} %broadcast.191), dimensions={1}, to_apply=%copy.43.reduce_sub_computation | reduce | bytes 1572866 | tf_op jit(solution)/shard_map/reshape | solution.py:54
  15.5 2.8 %reshape.168 = bf16[4,2,49152]{2,1,0:T(2,128)(2,1)} reshape(bf16[4,98304]{1,0:T(4,128)(2,1)} %reduce.2) | data formatting | bytes 1572864
  18.9 4.2 %all-to-all-start.1 = ((bf16[4,2,49152]{2,1,0:T(2,128)(2,1)}), bf16[4,2,49152]{2,1,0:T(2,128)(2,1)}, u32[]{:S(2)}, u32[]{:S(2)}) async-start(bf16[4,2,49152]{2,1,0:T(2,128)(2,1)} %reshape.168), calls=%async_computation.1 | async-start | bytes 1572864 | tf_op jit(solution)/shard_map/all_to_all | solution.py:53
  25.1 9.6 %all-to-all-done.1 = bf16[4,2,49152]{2,1,0:T(2,128)(2,1)} async-done(((bf16[4,2,49152]{2,1,0:T(2,128)(2,1)}), bf16[4,2,49152]{2,1,0:T(2,128)(2,1)}, u32[]{:S(2)}, u32[]{:S(2)}) %all-to-all-start.1) | async-done | bytes 786464 | tf_op jit(solution)/shard_map/all_to_all | solution.py:53
  34.8 3.7 %reshape.169 = bf16[4,1,98304]{2,1,0:T(2,128)(2,1)} reshape(bf16[4,2,49152]{2,1,0:T(2,128)(2,1)} %all-to-all-done.1) | data formatting | bytes 1572864
  38.5 3.6 %fusion.1 = f32[4,98304]{1,0:T(4,128)} fusion(bf16[4,1,98304]{2,1,0:T(2,128)(2,1)} %reshape.169, s32[4]{0:T(128)S(1)} %reduce), kind=kOutput, calls=%fused_computation.3 | convolution fusion | flops 3932176 | bytes 2359312 | tf_op jit(solution)/shard_map/dot_general | solution.py:67
  42.2 3.7 %reshape.163 = f32[512,768]{1,0:T(8,128)} reshape(f32[4,98304]{1,0:T(4,128)} %fusion.1) | data formatting | bytes 3145728 | tf_op jit(solution)/shard_map/convert_element_type | solution.py:91
  49.3 2.1 %convolution_convert_fusion.2 = bf16[512,2304]{1,0:T(8,128)(2,1)S(1)} fusion(bf16[768,2304]{1,0:T(8,128)(2,1)S(1)} %copy-done, f32[512,768]{1,0:T(8,128)S(1)} %copy-done.1, f32[512]{0:T(512)S(1)} %add_rsqrt_fusion.1, f32[512]{0:T(512)S(1)} %broadcast_multiply_fusion.1), kind=kOutput, calls=%fused_computation.17 | convolution fusion | flops 1814298624 | bytes 7475200 | tf_op jit(solution)/shard_map/dot_general | solution.py:74
  52.8 2.3 %copy.44 = bf16[512,768]{0,1:T(8,128)(2,1)} copy(bf16[512,768]{1,0:T(8,128)(2,1)} %get-tuple-element.7) | data formatting | bytes 1572864 | tf_op jit(solution)/shard_map/slice | solution.py:77
  55.1 2.3 %copy.46 = bf16[512,768]{0,1:T(8,128)(2,1)} copy(bf16[512,768]{1,0:T(8,128)(2,1)} %get-tuple-element.6) | data formatting | bytes 1572864 | tf_op jit(solution)/shard_map/slice | solution.py:75
  57.4 2.3 %copy.47 = bf16[512,768]{0,1:T(8,128)(2,1)} copy(bf16[512,768]{1,0:T(8,128)(2,1)} %get-tuple-element.5) | data formatting | bytes 1572864 | tf_op jit(solution)/shard_map/slice | solution.py:76
  59.7 11.2 %fusion.134 = (f32[12,512]{1,0:T(8,128)}, f32[12,512,512]{1,2,0:T(8,128)}) fusion(pred[512,512]{0,1:T(8,128)(4,1)} %bitcast_and_fusion, bf16[512,12,64]{0,2,1:T(8,128)(2,1)} %bitcast.139, bf16[512,12,64]{0,2,1:T(8,128)(2,1)} %bitcast.140), kind=kOutput, calls=%fused_computation.173 | convolution fusion | flops 415236608 | bytes 14442496 | tf_op jit(solution)/shard_map/sub | solution.py:86
  70.9 6.1 %fusion.31 = bf16[12,64,512]{2,1,0:T(8,128)(2,1)S(1)} fusion(bf16[512,12,64]{0,2,1:T(8,128)(2,1)} %bitcast.138, f32[12,512,512]{1,2,0:T(8,128)} %get-tuple-element.11, f32[12,512]{1,0:T(8,128)} %get-tuple-element.10), kind=kOutput, calls=%fused_computation.49 | convolution fusion | flops 409337856 | bytes 14180352 | tf_op jit(solution)/shard_map/hqk,khd->qhd/dot_general | solution.py:88
  80.6 13.5 %all_to_all.44 = bf16[4,32,768]{2,0,1:T(4,128)(2,1)} all-to-all(bf16[4,32,768]{2,0,1:T(4,128)(2,1)S(1)} %copy.49), channel_id=1, replica_groups=mesh['dp'=4,'expert'=8] {'dp','expert'}, dimensions={1} | all-to-all | bytes 393216 | tf_op jit(solution)/shard_map/all_to_all | solution.py:111
  95.8 9.2 %fusion.37 = bf16[128,1,768]{2,0,1:T(8,128)(2,1)} fusion(bf16[1,3072,768]{2,1,0:T(8,128)(2,1)} %param.17, bf16[128,768]{1,0:T(8,128)(2,1)} %reshape.159, bf16[1,768,3072]{2,1,0:T(8,128)(2,1)} %param.16), kind=kOutput, calls=%fused_computation.53 | convolution fusion | flops 1233616896 | bytes 9830400 | tf_op jit(solution)/shard_map/rkh,khd->rkd/dot_general | solution.py:114
  104.9 2.2 %reduce.3 = bf16[128,768]{1,0:T(8,128)(2,1)} reduce(bf16[128,1,768]{2,0,1:T(8,128)(2,1)} %fusion.37, bf16[]{:T(256)} %broadcast.191), dimensions={1}, to_apply=%copy.50.reduce_sub_computation | reduce | bytes 393218 | tf_op jit(solution)/shard_map/convert_element_type | solution.py:116
  108.9 3.4 %all-to-all-start.3 = ((bf16[32,2,1536]{2,1,0:T(2,128)(2,1)}), bf16[32,2,1536]{2,1,0:T(2,128)(2,1)}, u32[]{:S(2)}, u32[]{:S(2)}) async-start(bf16[32,2,1536]{2,1,0:T(2,128)(2,1)} %reshape.170), calls=%async_computation.3 | async-start | bytes 393216 | tf_op jit(solution)/shard_map/all_to_all | solution.py:117
  114.6 5.9 %all-to-all-done.3 = bf16[32,2,1536]{2,1,0:T(2,128)(2,1)} async-done(((bf16[32,2,1536]{2,1,0:T(2,128)(2,1)}), bf16[32,2,1536]{2,1,0:T(2,128)(2,1)}, u32[]{:S(2)}, u32[]{:S(2)}) %all-to-all-start.3) | async-done | bytes 196640 | tf_op jit(solution)/shard_map/all_to_all | solution.py:117
  120.6 2.2 %reshape.171 = bf16[128,1,768]{2,1,0:T(2,128)(2,1)} reshape(bf16[32,2,1536]{2,1,0:T(2,128)(2,1)} %all-to-all-done.3) | data formatting | bytes 393216
  122.8 2.7 %reduce.1 = bf16[128,768]{1,0:T(8,128)(2,1)} reduce(bf16[128,1,768]{2,1,0:T(2,128)(2,1)} %reshape.171, bf16[]{:T(256)} %constant.140), dimensions={1}, to_apply=%all_to_all.36.reduce_sub_computation | reduce | bytes 393218 | tf_op jit(solution)/shard_map/all_to_all | solution.py:117
  127.2 2.5 %fusion.16 = bf16[512,768]{1,0:T(8,128)(2,1)} fusion(bf16[512,768]{1,0:T(8,128)(2,1)} %copy-done.3, bf16[32,4,1,768]{3,1,0,2:T(4,128)(2,1)} %all_to_all.37, pred[4,512]{1,0:T(4,128)(4,1)S(1)} %iota_compare_fusion, bf16[512,32]{0,1:T(8,128)(2,1)} %divide_convert_fusion.4), kind=kOutput, calls=%fused_computation.26 | convolution fusion | flops 101908480 | bytes 1804288 | tf_op jit(solution)/shard_map/ste,sed->td/dot_general | solution.py:119
  (57 shorter events, 20.8 us)
Async XLA Ops:
  0.0 49.3 %copy-start = (bf16[768,2304]{1,0:T(8,128)(2,1)S(1)}, bf16[768,2304]{1,0:T(8,128)(2,1)}, u32[]{:S(2)}) copy-start(bf16[768,2304]{1,0:T(8,128)(2,1)} %param.13) | copy-start | bytes 10616836
  1.9 17.0 %all-to-all-start = ((s32[4,1,1]{2,1,0:T(1,128)}), s32[4,1,1]{2,1,0:T(1,128)S(1)}, u32[]{:S(2)}, u32[]{:S(2)}) async-start(s32[4,1,1]{2,1,0:T(1,128)} %copy.42), calls=%async_computation | async-start | bytes 4096 | tf_op jit(solution)/shard_map/all_to_all | solution.py:60
  11.9 6.4 %copy-start.7 = (s32[4,4]{1,0:T(4,128)S(1)}, s32[4,4]{1,0:T(4,128)}, u32[]{:S(2)}) copy-start(s32[4,4]{1,0:T(4,128)} %param.12) | copy-start | bytes 196
  15.4 7.6 %copy-start.6 = (s32[512]{0:T(512)S(1)}, s32[512]{0:T(512)}, u32[]{:S(2)}) copy-start(s32[512]{0:T(512)} %param.11) | copy-start | bytes 6148
  18.9 15.9 %all-to-all-start.1 = ((bf16[4,2,49152]{2,1,0:T(2,128)(2,1)}), bf16[4,2,49152]{2,1,0:T(2,128)(2,1)}, u32[]{:S(2)}, u32[]{:S(2)}) async-start(bf16[4,2,49152]{2,1,0:T(2,128)(2,1)} %reshape.168), calls=%async_computation.1 | async-start | bytes 1572864 | tf_op jit(solution)/shard_map/all_to_all | solution.py:53
  47.4 1.9 %copy-start.1 = (f32[512,768]{1,0:T(8,128)S(1)}, f32[512,768]{1,0:T(8,128)}, u32[]{:S(2)}) copy-start(f32[512,768]{1,0:T(8,128)} %reshape.163) | copy-start | bytes 4718596
  70.9 6.1 %copy-start.2 = (f32[512,768]{1,0:T(8,128)S(1)}, f32[512,768]{1,0:T(8,128)}, u32[]{:S(2)}) copy-start(f32[512,768]{1,0:T(8,128)} %reshape.163) | copy-start | bytes 4718596
  70.9 6.1 %copy-start.8 = (bf16[768,768]{1,0:T(8,128)(2,1)S(1)}, bf16[768,768]{1,0:T(8,128)(2,1)}, u32[]{:S(2)}) copy-start(bf16[768,768]{1,0:T(8,128)(2,1)} %param.14) | copy-start | bytes 3538948
  78.0 1.2 copy-start.3
  78.0 0.8 copy-start.5
  79.2 1.0 copy-start.4
  108.9 11.7 %all-to-all-start.3 = ((bf16[32,2,1536]{2,1,0:T(2,128)(2,1)}), bf16[32,2,1536]{2,1,0:T(2,128)(2,1)}, u32[]{:S(2)}, u32[]{:S(2)}) async-start(bf16[32,2,1536]{2,1,0:T(2,128)(2,1)} %reshape.170), calls=%async_computation.3 | async-start | bytes 393216 | tf_op jit(solution)/shard_map/all_to_all | solution.py:117
where the time goes:
time: 131 us; the launch traced here: 130 us
  matrix products  39.4 us (30%)
  local copies, waits for them, and re-layouts  31.7 us (24%)
  other arithmetic  17.4 us (13%)
  waiting for transfers between devices  15.6 us (12%)
  blocking collectives  13.5 us (10%)
  starting transfers between devices  11.9 us (9%)
    all_to_all x1, blocking collectives, per_device(): lax.all_to_all(slot_in, ('dp', 'expert'), split_axis=1, concat_axis=0, ti...  13.5 us
    sub x1, matrix products, per_device(): raised = jnp.exp(scores - jnp.max(scores, axis=2, keepdims=True))  11.2 us
    unnamed x22, local copies, waits for them, and re-layouts  10.7 us
    all_to_all x1, waiting for transfers between devices, per_device(): lax.all_to_all(send_rows.reshape(data_count, peer_cap, block_rows * width...  9.65 us
    dot_general x1, matrix products, per_device(): jnp.einsum('rkh,khd->rkd', inner, expert_out, preferred_element_type=jnp....  9.17 us
    dot_general x1, matrix products, per_device(): jnp.einsum('hqk,khd->qhd', weights, value_rows, preferred_element_type=jn...  6.08 us
    all_to_all x1, waiting for transfers between devices, per_device(): lax.all_to_all(produced, ('dp', 'expert'), split_axis=0, concat_axis=1, t...  5.92 us
    all_to_all x1, starting transfers between devices, per_device(): lax.all_to_all(send_place.reshape(data_count, peer_cap), 'dp', split_axis...  4.26 us
  transfers between devices with their start and end apart: 3, of which 2 were waited for; matrix products, arithmetic and copies ran while one was open for 13% of the time, Pallas kernels for 0%

commit v1 on v0

--- a/solution.py
+++ b/solution.py
@@ -114,7 +114,15 @@
     produced = jnp.einsum(
         "rkh,khd->rkd", inner, expert_out, preferred_element_type=jnp.float32
     ).astype(jnp.bfloat16)
-    returned = lax.all_to_all(produced, ("dp", "expert"), split_axis=0, concat_axis=1, tiled=True)
+    returned = jnp.concatenate(
+        lax.all_to_all(
+            jnp.stack(jnp.split(produced, lax.axis_size(("dp", "expert")), axis=0)),
+            ("dp", "expert"),
+            0,
+            0,
+        ),
+        axis=1,
+    )
     masked_combine = jnp.where(member[:, :, None], combine[None], jnp.zeros((), jnp.bfloat16))
     mixture = jnp.einsum(
         "ste,sed->td", masked_combine, returned, preferred_element_type=jnp.float32

time: 131 us -> 164 us (1.25); the launches traced: 130 us -> 161 us
  local copies, waits for them, and re-layouts: 31.7 us -> 67.8 us
  other arithmetic: 17.4 us -> 12.4 us
    unnamed x22 -> x51, local copies, waits for them, and re-layouts: 10.7 us -> 47.2 us
    all_to_all x1 -> x0, other arithmetic: 2.74 us -> none  [per_device(): lax.all_to_all(produced, ('dp', 'expert'), split_axis=0, concat_axis=1, t...]
    convert_element_type x1 -> x0, other arithmetic: 2.25 us -> none  [per_device(): produced = jnp.einsum('rkh,khd->rkd', inner, expert_out, preferred_elemen...]
    all_to_all x1 -> x0, local copies, waits for them, and re-layouts: 1.65 us -> none  [per_device(): lax.all_to_all(produced, ('dp', 'expert'), split_axis=0, concat_axis=1, t...]
  transfers between devices with their start and end apart: 3 -> 3, of which waited for: 2 -> 2; matrix products, arithmetic and copies ran while one was open for 13% -> 11% of each run, Pallas kernels for 0% -> 0%
where the time goes in v1:
time: 164 us; the launch traced here: 161 us
  local copies, waits for them, and re-layouts  67.8 us (41%)
  matrix products  39.4 us (24%)
  waiting for transfers between devices  15.6 us (10%)
  blocking collectives  13.5 us (8%)
  other arithmetic  12.4 us (8%)
  starting transfers between devices  11.9 us (7%)
    unnamed x51, local copies, waits for them, and re-layouts  47.2 us
    all_to_all x1, blocking collectives, per_device(): lax.all_to_all(slot_in, ('dp', 'expert'), split_axis=1, concat_axis=0, ti...  13.5 us
    sub x1, matrix products, per_device(): raised = jnp.exp(scores - jnp.max(scores, axis=2, keepdims=True))  11.2 us
    all_to_all x1, waiting for transfers between devices, per_device(): lax.all_to_all(send_rows.reshape(data_count, peer_cap, block_rows * width...  9.65 us
    dot_general x1, matrix products, per_device(): jnp.einsum('rkh,khd->rkd', inner, expert_out, preferred_element_type=jnp....  9.17 us
    dot_general x1, matrix products, per_device(): jnp.einsum('hqk,khd->qhd', weights, value_rows, preferred_element_type=jn...  6.08 us
    all_to_all x1, waiting for transfers between devices, per_device(): lax.all_to_all(jnp.stack(jnp.split(produced, lax.axis_size(('dp', 'expert...  5.92 us
    all_to_all x1, starting transfers between devices, per_device(): lax.all_to_all(send_place.reshape(data_count, peer_cap), 'dp', split_axis...  4.26 us
  transfers between devices with their start and end apart: 3, of which 2 were waited for; matrix products, arithmetic and copies ran while one was open for 11% of the time, Pallas kernels for 0%

profile of v1, /device:TPU:0, one launch (start us, length us, event | category | flops | bytes accessed | tf_op | source)
XLA Modules:
  0.0 160.8 jit_solution(4542092990415758179)
XLA Ops:
  1.9 4.3 %all-to-all-start = ((s32[4,1,1]{2,1,0:T(1,128)}), s32[4,1,1]{2,1,0:T(1,128)S(1)}, u32[]{:S(2)}, u32[]{:S(2)}) async-start(s32[4,1,1]{2,1,0:T(1,128)} %copy.41), calls=%async_computation | async-start | bytes 4096 | tf_op jit(solution)/shard_map/all_to_all | solution.py:60
  6.2 2.6 %reshape.157 = bf16[4,98304]{1,0:T(4,128)(2,1)} reshape(bf16[512,768]{1,0:T(8,128)(2,1)} %param.9) | data formatting | bytes 1572864 | tf_op jit(solution)/shard_map/reshape | solution.py:47
  8.8 2.6 %fusion.2 = bf16[4,1,98304]{2,0,1:T(4,128)(2,1)} fusion(bf16[4,98304]{1,0:T(4,128)(2,1)} %reshape.157, s32[4]{0:T(128)S(1)} %add.54), kind=kOutput, calls=%fused_computation.4 | convolution fusion | flops 3538960 | bytes 1572880 | tf_op jit(solution)/shard_map/dot_general | solution.py:48
  11.9 3.5 %reduce.1 = bf16[4,98304]{1,0:T(4,128)(2,1)} reduce(bf16[4,1,98304]{2,0,1:T(4,128)(2,1)} %fusion.2, bf16[]{:T(256)} %broadcast.190), dimensions={1}, to_apply=%copy.42.reduce_sub_computation | reduce | bytes 1572866 | tf_op jit(solution)/shard_map/reshape | solution.py:54
  15.4 2.8 %reshape.175 = bf16[4,2,49152]{2,1,0:T(2,128)(2,1)} reshape(bf16[4,98304]{1,0:T(4,128)(2,1)} %reduce.1) | data formatting | bytes 1572864
  18.9 4.2 %all-to-all-start.1 = ((bf16[4,2,49152]{2,1,0:T(2,128)(2,1)}), bf16[4,2,49152]{2,1,0:T(2,128)(2,1)}, u32[]{:S(2)}, u32[]{:S(2)}) async-start(bf16[4,2,49152]{2,1,0:T(2,128)(2,1)} %reshape.175), calls=%async_computation.1 | async-start | bytes 1572864 | tf_op jit(solution)/shard_map/all_to_all | solution.py:53
  25.1 9.6 %all-to-all-done.1 = bf16[4,2,49152]{2,1,0:T(2,128)(2,1)} async-done(((bf16[4,2,49152]{2,1,0:T(2,128)(2,1)}), bf16[4,2,49152]{2,1,0:T(2,128)(2,1)}, u32[]{:S(2)}, u32[]{:S(2)}) %all-to-all-start.1) | async-done | bytes 786464 | tf_op jit(solution)/shard_map/all_to_all | solution.py:53
  34.8 3.7 %reshape.176 = bf16[4,1,98304]{2,1,0:T(2,128)(2,1)} reshape(bf16[4,2,49152]{2,1,0:T(2,128)(2,1)} %all-to-all-done.1) | data formatting | bytes 1572864
  38.5 3.6 %fusion.1 = f32[4,98304]{1,0:T(4,128)} fusion(bf16[4,1,98304]{2,1,0:T(2,128)(2,1)} %reshape.176, s32[4]{0:T(128)S(1)} %reduce), kind=kOutput, calls=%fused_computation.3 | convolution fusion | flops 3932176 | bytes 2359312 | tf_op jit(solution)/shard_map/dot_general | solution.py:67
  42.1 3.7 %reshape.171 = f32[512,768]{1,0:T(8,128)} reshape(f32[4,98304]{1,0:T(4,128)} %fusion.1) | data formatting | bytes 3145728 | tf_op jit(solution)/shard_map/convert_element_type | solution.py:91
  45.8 1.6 reduce_sum.74
  47.4 1.8 %multiply_reduce_fusion = f32[512]{0:T(512)S(1)} fusion(f32[512,768]{1,0:T(8,128)} %reshape.171, f32[512]{0:T(512)S(1)} %broadcast_multiply_fusion.1), kind=kLoop, calls=%fused_computation.46 | loop fusion | flops 1179136 | bytes 1576960 | tf_op jit(solution)/shard_map/reduce_sum | solution.py:15
  49.2 2.1 %convolution_convert_fusion.2 = bf16[512,2304]{1,0:T(8,128)(2,1)S(1)} fusion(bf16[768,2304]{1,0:T(8,128)(2,1)S(1)} %copy-done, f32[512,768]{1,0:T(8,128)S(1)} %copy-done.1, f32[512]{0:T(512)S(1)} %add_rsqrt_fusion.1, f32[512]{0:T(512)S(1)} %broadcast_multiply_fusion.1), kind=kOutput, calls=%fused_computation.17 | convolution fusion | flops 1814298624 | bytes 7475200 | tf_op jit(solution)/shard_map/dot_general | solution.py:74
  52.8 2.3 %copy.43 = bf16[512,768]{0,1:T(8,128)(2,1)} copy(bf16[512,768]{1,0:T(8,128)(2,1)} %get-tuple-element.7) | data formatting | bytes 1572864 | tf_op jit(solution)/shard_map/slice | solution.py:77
  55.1 2.3 %copy.45 = bf16[512,768]{0,1:T(8,128)(2,1)} copy(bf16[512,768]{1,0:T(8,128)(2,1)} %get-tuple-element.6) | data formatting | bytes 1572864 | tf_op jit(solution)/shard_map/slice | solution.py:75
  57.4 2.3 %copy.46 = bf16[512,768]{0,1:T(8,128)(2,1)} copy(bf16[512,768]{1,0:T(8,128)(2,1)} %get-tuple-element.5) | data formatting | bytes 1572864 | tf_op jit(solution)/shard_map/slice | solution.py:76
  59.7 11.2 %fusion.133 = (f32[12,512]{1,0:T(8,128)}, f32[12,512,512]{1,2,0:T(8,128)}) fusion(pred[512,512]{0,1:T(8,128)(4,1)} %bitcast_and_fusion, bf16[512,12,64]{0,2,1:T(8,128)(2,1)} %bitcast.265, bf16[512,12,64]{0,2,1:T(8,128)(2,1)} %bitcast.266), kind=kOutput, calls=%fused_computation.236 | convolution fusion | flops 415236608 | bytes 14442496 | tf_op jit(solution)/shard_map/sub | solution.py:86
  70.9 6.1 %fusion.31 = bf16[12,64,512]{2,1,0:T(8,128)(2,1)S(1)} fusion(bf16[512,12,64]{0,2,1:T(8,128)(2,1)} %bitcast.264, f32[12,512,512]{1,2,0:T(8,128)} %get-tuple-element.11, f32[12,512]{1,0:T(8,128)} %get-tuple-element.10), kind=kOutput, calls=%fused_computation.49 | convolution fusion | flops 409337856 | bytes 14180352 | tf_op jit(solution)/shard_map/hqk,khd->qhd/dot_general | solution.py:88
  80.5 13.5 %all_to_all.31 = bf16[4,32,768]{2,0,1:T(4,128)(2,1)} all-to-all(bf16[4,32,768]{2,0,1:T(4,128)(2,1)S(1)} %copy.48), channel_id=1, replica_groups=mesh['dp'=4,'expert'=8] {'dp','expert'}, dimensions={1} | all-to-all | bytes 393216 | tf_op jit(solution)/shard_map/all_to_all | solution.py:111
  94.1 1.7 %reshape.165 = bf16[128,768]{1,0:T(8,128)(2,1)} reshape(bf16[32,4,1,768]{3,1,0,2:T(4,128)(2,1)} %bitcast.267) | data formatting | bytes 393216 | tf_op jit(solution)/shard_map/reshape.1
  95.7 9.2 %fusion.37 = bf16[128,1,768]{2,0,1:T(8,128)(2,1)} fusion(bf16[1,3072,768]{2,1,0:T(8,128)(2,1)} %param.17, bf16[128,768]{1,0:T(8,128)(2,1)} %reshape.165, bf16[1,768,3072]{2,1,0:T(8,128)(2,1)} %param.16), kind=kOutput, calls=%fused_computation.53 | convolution fusion | flops 1233616896 | bytes 9830400 | tf_op jit(solution)/shard_map/rkh,khd->rkd/dot_general | solution.py:114
  146.6 3.4 %all-to-all-start.3 = ((bf16[32,4,1,768]{3,1,2,0:T(4,128)(2,1)}), bf16[32,4,1,768]{3,1,2,0:T(4,128)(2,1)}, u32[]{:S(2)}, u32[]{:S(2)}) async-start(bf16[32,4,1,768]{3,1,2,0:T(4,128)(2,1)} %constant_dynamic-update-slice_fusion), calls=%async_computation.3 | async-start | bytes 393216 | tf_op jit(solution)/shard_map/all_to_all | solution.py:118
  152.3 5.9 %all-to-all-done.3 = bf16[32,4,1,768]{3,1,2,0:T(4,128)(2,1)} async-done(((bf16[32,4,1,768]{3,1,2,0:T(4,128)(2,1)}), bf16[32,4,1,768]{3,1,2,0:T(4,128)(2,1)}, u32[]{:S(2)}, u32[]{:S(2)}) %all-to-all-start.3) | async-done | bytes 196640 | tf_op jit(solution)/shard_map/all_to_all | solution.py:118
  158.3 2.5 %fusion.16 = bf16[512,768]{1,0:T(8,128)(2,1)} fusion(bf16[512,768]{1,0:T(8,128)(2,1)} %copy-done.3, bf16[4,32,768]{2,0,1:T(4,128)(2,1)} %bitcast.59, pred[4,512]{1,0:T(4,128)(4,1)S(1)} %iota_compare_fusion, bf16[512,32]{0,1:T(8,128)(2,1)} %divide_convert_fusion.4), kind=kOutput, calls=%fused_computation.26 | convolution fusion | flops 101908480 | bytes 1804288 | tf_op jit(solution)/shard_map/ste,sed->td/dot_general | solution.py:127
  (84 shorter events, 54.1 us)
Async XLA Ops:
  0.0 49.2 %copy-start = (bf16[768,2304]{1,0:T(8,128)(2,1)S(1)}, bf16[768,2304]{1,0:T(8,128)(2,1)}, u32[]{:S(2)}) copy-start(bf16[768,2304]{1,0:T(8,128)(2,1)} %param.13) | copy-start | bytes 10616836
  1.9 16.9 %all-to-all-start = ((s32[4,1,1]{2,1,0:T(1,128)}), s32[4,1,1]{2,1,0:T(1,128)S(1)}, u32[]{:S(2)}, u32[]{:S(2)}) async-start(s32[4,1,1]{2,1,0:T(1,128)} %copy.41), calls=%async_computation | async-start | bytes 4096 | tf_op jit(solution)/shard_map/all_to_all | solution.py:60
  11.9 6.4 %copy-start.7 = (s32[4,4]{1,0:T(4,128)S(1)}, s32[4,4]{1,0:T(4,128)}, u32[]{:S(2)}) copy-start(s32[4,4]{1,0:T(4,128)} %param.12) | copy-start | bytes 196
  15.4 7.6 %copy-start.6 = (s32[512]{0:T(512)S(1)}, s32[512]{0:T(512)}, u32[]{:S(2)}) copy-start(s32[512]{0:T(512)} %param.11) | copy-start | bytes 6148
  18.9 15.9 %all-to-all-start.1 = ((bf16[4,2,49152]{2,1,0:T(2,128)(2,1)}), bf16[4,2,49152]{2,1,0:T(2,128)(2,1)}, u32[]{:S(2)}, u32[]{:S(2)}) async-start(bf16[4,2,49152]{2,1,0:T(2,128)(2,1)} %reshape.175), calls=%async_computation.1 | async-start | bytes 1572864 | tf_op jit(solution)/shard_map/all_to_all | solution.py:53
  47.4 1.9 %copy-start.1 = (f32[512,768]{1,0:T(8,128)S(1)}, f32[512,768]{1,0:T(8,128)}, u32[]{:S(2)}) copy-start(f32[512,768]{1,0:T(8,128)} %reshape.171) | copy-start | bytes 4718596
  70.9 6.1 %copy-start.2 = (f32[512,768]{1,0:T(8,128)S(1)}, f32[512,768]{1,0:T(8,128)}, u32[]{:S(2)}) copy-start(f32[512,768]{1,0:T(8,128)} %reshape.171) | copy-start | bytes 4718596
  70.9 6.1 %copy-start.8 = (bf16[768,768]{1,0:T(8,128)(2,1)S(1)}, bf16[768,768]{1,0:T(8,128)(2,1)}, u32[]{:S(2)}) copy-start(bf16[768,768]{1,0:T(8,128)(2,1)} %param.14) | copy-start | bytes 3538948
  77.9 1.2 copy-start.3
  77.9 0.8 copy-start.5
  79.1 1.0 copy-start.4
  146.6 11.7 %all-to-all-start.3 = ((bf16[32,4,1,768]{3,1,2,0:T(4,128)(2,1)}), bf16[32,4,1,768]{3,1,2,0:T(4,128)(2,1)}, u32[]{:S(2)}, u32[]{:S(2)}) async-start(bf16[32,4,1,768]{3,1,2,0:T(4,128)(2,1)} %constant_dynamic-update-slice_fusion), calls=%async_computation.3 | async-start | bytes 393216 | tf_op jit(solution)/shard_map/all_to_all | solution.py:118
